TPU v7x, 32 devices: a whole 2x2x4 slice. The times are simulated.
32 devices in a mesh: dp: 4 (over y, x), ctx: 8 (over z, core).
Axes of the slice: x: 2, y: 2, z: 4, core: 2. Of those that a mesh axis runs over, the one named last changes fastest.
Arguments:
- tokens: bfloat16 [4, 1024, 1536], P('dp', 'ctx'), may hold values from -6 to 6
- positions: int32 [4, 1024], P('dp', 'ctx'), may hold values from 0 to 3071, as said below
- block_order: int32 [16], replicated, may hold values from 0 to 15, as said below
- cotangent: bfloat16 [4, 1024, 1536], P('dp', 'ctx'), may hold values from -6 to 6
- gain_attn: bfloat16 [1536], P('dp'), may hold values from 0.099609375 to 1.8984375
- w_qkv: bfloat16 [1536, 2048], P('dp'), may hold values from -0.15625 to 0.15625
- b_qkv: bfloat16 [2048], P('dp'), may hold values from -3 to 3
- w_out: bfloat16 [1536, 1536], P('dp'), may hold values from -1.75 to 1.75
- gain_mlp: bfloat16 [1536], P('dp'), may hold values from 0.099609375 to 1.8984375
- w_gate: bfloat16 [1536, 8960], P('dp'), may hold values from -0.15625 to 0.15625
- w_up: bfloat16 [1536, 8960], P('dp'), may hold values from -0.15625 to 0.15625
- w_down: bfloat16 [8960, 1536], P('dp'), may hold values from -0.0625 to 0.0625
Outputs:
- block_out: bfloat16 [4, 1024, 1536], P('dp', 'ctx')
- grad_tokens: float32 [4, 1024, 1536], P('dp', 'ctx')
- grad_gain_attn: float32 [1536], P(('dp', 'ctx'))
- grad_w_qkv: float32 [1536, 2048], P(('dp', 'ctx'))
- grad_b_qkv: float32 [2048], P(('dp', 'ctx'))
- grad_w_out: float32 [1536, 1536], P(('dp', 'ctx'))
- grad_gain_mlp: float32 [1536], P(('dp', 'ctx'))
- grad_w_gate: float32 [1536, 8960], P(('dp', 'ctx'))
- grad_w_up: float32 [1536, 8960], P(('dp', 'ctx'))
- grad_w_down: float32 [8960, 1536], P(('dp', 'ctx'))
Inputs may be any that keep to these rules, and one draw needn't show every extreme that they name: A permutation in which entries 2c and 2c + 1 always add up to 15; the device of index c along ctx stores, as its first and its second 64 tokens of every sequence, that sequence's sub-blocks block_order[2c] and block_order[2c + 1]. positions[s, t] is an offset of sequence s, from 0 to 2048, plus the index idx(t) of the token stored at place t; the first sequence's offset is 0 and the last one's 2 * 1024.
All inputs are finite; a program needn't handle non-finite values.
Results may differ from a plain program's by a relative error of at most 0.02.
Values may be sent and summed in bfloat16 or wider, within the bound.
No kernel may reach another device: no remote copies, remote signals or barrier semaphores. Data moves between devices by JAX's collectives and lax.ppermute only.
A program may use at most 576 MiB of HBM per device.

v0:
```python
import math

import jax
import jax.numpy as jnp
from jax import lax
from jax.sharding import PartitionSpec as P

HEADS = 12
KV_HEADS = 2
HEAD_DIM = 128


rope_base = 1000000.0
norm_eps = 1e-06
masked_score = -1e30


def from_behind(value, axis, steps):
    count = lax.axis_size(axis)
    pairs = [(source, (source + steps) % count) for source in range(count)]
    return lax.ppermute(value, axis, pairs)


def normalize(rows_in, gain):
    inverse = lax.rsqrt(jnp.mean(rows_in * rows_in, axis=-1, keepdims=True) + norm_eps)
    normed = rows_in * inverse
    return (normed, inverse, (normed * gain.astype(jnp.float32)).astype(jnp.bfloat16))


def normalize_back(grad_out, normed, inverse, gain):
    scaled = grad_out * gain.astype(jnp.float32)
    grad_rows = inverse * (scaled - normed * jnp.mean(scaled * normed, axis=-1, keepdims=True))
    return (grad_rows, jnp.sum(grad_out * normed, axis=0))


def rope_tables(token_positions, head_dim):
    half_dim = head_dim // 2
    half_steps = jnp.arange(half_dim, dtype=jnp.float32)
    frequency = jnp.exp(-math.log(rope_base) * (2.0 * half_steps / head_dim))
    angles = token_positions.astype(jnp.float32)[:, None] * frequency[None, :]
    return (jnp.cos(angles), jnp.sin(angles))


def rotate(head_rows, cosines, sines):
    half_dim = head_rows.shape[-1] // 2
    front_half = head_rows[..., :half_dim]
    back_half = head_rows[..., half_dim:]
    cosine_part = cosines[:, None, :]
    sine_part = sines[:, None, :]
    return jnp.concatenate(
        [
            front_half * cosine_part - back_half * sine_part,
            back_half * cosine_part + front_half * sine_part,
        ],
        axis=-1,
    )


def unrotate(grad_rows, cosines, sines):
    half_dim = grad_rows.shape[-1] // 2
    front_half = grad_rows[..., :half_dim]
    back_half = grad_rows[..., half_dim:]
    cosine_part = cosines[:, None, :]
    sine_part = sines[:, None, :]
    return jnp.concatenate(
        [
            front_half * cosine_part + back_half * sine_part,
            back_half * cosine_part - front_half * sine_part,
        ],
        axis=-1,
    )


def logical_index(places, block_order, sub_len):
    slot_index = places // sub_len
    slot_match = slot_index[:, None] == jnp.arange(block_order.shape[0], dtype=jnp.int32)[None, :]
    blocks = jnp.sum(jnp.where(slot_match, block_order[None, :], 0), axis=1)
    return blocks * sub_len + places % sub_len


def block_scores(queries, key_rows, allowed, score_scale):
    scores = (
        jnp.einsum("skgtd,sukd->skgtu", queries, key_rows, preferred_element_type=jnp.float32)
        * score_scale
    )
    return jnp.where(allowed, scores, masked_score)


def attend(softmax_state, queries, kv_pair, allowed, score_scale):
    running, total_mass, summed = softmax_state
    scores = block_scores(queries, kv_pair[0], allowed, score_scale)
    newest = jnp.maximum(running, jnp.max(scores, axis=-1))
    factor = jnp.exp(running - newest)
    unscaled = jnp.exp(scores - newest[..., None])
    total_mass = total_mass * factor + jnp.sum(unscaled, axis=-1)
    summed = summed * factor[..., None] + jnp.einsum(
        "skgtu,sukd->skgtd",
        unscaled.astype(jnp.bfloat16),
        kv_pair[1],
        preferred_element_type=jnp.float32,
    )
    return (newest, total_mass, summed)


def attend_back(queries, kv_pair, allowed, log_total, grad_heads, delta, score_scale):
    scores = block_scores(queries, kv_pair[0], allowed, score_scale)
    probs_full = jnp.where(allowed, jnp.exp(scores - log_total[..., None]), 0.0)
    grad_probs = jnp.einsum(
        "skgtd,sukd->skgtu", grad_heads, kv_pair[1], preferred_element_type=jnp.float32
    )
    grad_scores = (probs_full * (grad_probs - delta[..., None])).astype(jnp.bfloat16)
    grad_query = (
        jnp.einsum("skgtu,sukd->skgtd", grad_scores, kv_pair[0], preferred_element_type=jnp.float32)
        * score_scale
    )
    grad_key = (
        jnp.einsum("skgtu,skgtd->sukd", grad_scores, queries, preferred_element_type=jnp.float32)
        * score_scale
    )
    grad_value = jnp.einsum(
        "skgtu,skgtd->sukd",
        probs_full.astype(jnp.bfloat16),
        grad_heads,
        preferred_element_type=jnp.float32,
    )
    return (grad_query, jnp.stack([grad_key, grad_value]))


def body(
    tokens,
    positions,
    block_order,
    cotangent,
    gain_attn,
    w_qkv,
    b_qkv,
    w_out,
    gain_mlp,
    w_gate,
    w_up,
    w_down,
):
    seq_count, tok_count, width = tokens.shape
    row_count = seq_count * tok_count
    ctx_count = lax.axis_size("ctx")
    ctx_place = lax.axis_index("ctx")
    groups = HEADS // KV_HEADS
    query_width = HEADS * HEAD_DIM
    kv_width = KV_HEADS * HEAD_DIM
    proj_width = query_width + 2 * kv_width
    score_scale = 1.0 / math.sqrt(HEAD_DIM)
    sub_len = tok_count // 2
    local_places = jnp.arange(tok_count, dtype=jnp.int32)
    own_index = logical_index(ctx_place * tok_count + local_places, block_order, sub_len)

    def visible(places):
        return logical_index(places, block_order, sub_len)[None, :] <= own_index[:, None]

    gain_one, qkv_full, bias_full, out_full = (
        lax.all_gather(gain_attn, "dp", axis=0, tiled=True),
        lax.all_gather(w_qkv, "dp", axis=0, tiled=True),
        lax.all_gather(b_qkv, "dp", axis=0, tiled=True),
        lax.all_gather(w_out, "dp", axis=0, tiled=True),
    )
    inputs = tokens.reshape(row_count, width).astype(jnp.float32)
    normed_one, inverse_one, hidden_one = normalize(inputs, gain_one)
    projected = jnp.dot(
        hidden_one, qkv_full, preferred_element_type=jnp.float32
    ) + bias_full.astype(jnp.float32)
    cosines, sines = rope_tables(positions.reshape(row_count), HEAD_DIM)
    query_rot = rotate(
        projected[:, :query_width].reshape(row_count, HEADS, HEAD_DIM), cosines, sines
    )
    key_rot = rotate(
        projected[:, query_width : query_width + kv_width].reshape(row_count, KV_HEADS, HEAD_DIM),
        cosines,
        sines,
    )
    value_part = projected[:, query_width + kv_width :]
    queries = (
        query_rot.astype(jnp.bfloat16)
        .reshape(seq_count, tok_count, KV_HEADS, groups, HEAD_DIM)
        .transpose(0, 2, 3, 1, 4)
    )
    key_rows = key_rot.astype(jnp.bfloat16).reshape(seq_count, tok_count, KV_HEADS, HEAD_DIM)
    value_rows = value_part.astype(jnp.bfloat16).reshape(seq_count, tok_count, KV_HEADS, HEAD_DIM)
    kv_pair = jnp.stack([key_rows, value_rows])
    start_state = (
        jnp.full((seq_count, KV_HEADS, groups, tok_count), masked_score, jnp.float32),
        jnp.zeros((seq_count, KV_HEADS, groups, tok_count), jnp.float32),
        jnp.zeros((seq_count, KV_HEADS, groups, tok_count, HEAD_DIM), jnp.float32),
    )

    def cycle_step(step_index, loop_carry):
        softmax_state, pair_now = loop_carry
        source = (ctx_place - step_index) % ctx_count
        allowed = visible(source * tok_count + local_places)
        softmax_state = attend(softmax_state, queries, pair_now, allowed, score_scale)
        pair_now = from_behind(pair_now, "ctx", 1)
        return (softmax_state, pair_now)

    softmax_state, pair_last = lax.fori_loop(0, ctx_count - 1, cycle_step, (start_state, kv_pair))
    source_last = (ctx_place - (ctx_count - 1)) % ctx_count
    softmax_state = attend(
        softmax_state,
        queries,
        pair_last,
        visible(source_last * tok_count + local_places),
        score_scale,
    )
    running, total_mass, summed = softmax_state
    attn_rows = summed / total_mass[..., None]
    log_total = running + jnp.log(total_mass)
    attn_flat = (
        attn_rows.astype(jnp.bfloat16).transpose(0, 3, 1, 2, 4).reshape(row_count, query_width)
    )
    middle = inputs + jnp.dot(attn_flat, out_full, preferred_element_type=jnp.float32)
    gain_two, gate_full, up_full, down_full = (
        lax.all_gather(gain_mlp, "dp", axis=0, tiled=True),
        lax.all_gather(w_gate, "dp", axis=0, tiled=True),
        lax.all_gather(w_up, "dp", axis=0, tiled=True),
        lax.all_gather(w_down, "dp", axis=0, tiled=True),
    )
    normed_two, inverse_two, hidden_two = normalize(middle, gain_two)
    gate_values = jnp.dot(hidden_two, gate_full, preferred_element_type=jnp.float32)
    up_values = jnp.dot(hidden_two, up_full, preferred_element_type=jnp.float32)
    sigmoid_gate = jax.nn.sigmoid(gate_values)
    activated = (gate_values * sigmoid_gate * up_values).astype(jnp.bfloat16)
    result = middle + jnp.dot(activated, down_full, preferred_element_type=jnp.float32)
    block_out = result.astype(jnp.bfloat16).reshape(seq_count, tok_count, width)
    grad_top = cotangent.reshape(row_count, width)
    gain_two_b, gate_b, up_b, down_b = (
        lax.all_gather(gain_mlp, "dp", axis=0, tiled=True),
        lax.all_gather(w_gate, "dp", axis=0, tiled=True),
        lax.all_gather(w_up, "dp", axis=0, tiled=True),
        lax.all_gather(w_down, "dp", axis=0, tiled=True),
    )
    left_part = activated
    down_share = lax.psum_scatter(
        jnp.einsum("rf,rd->fd", left_part, grad_top, preferred_element_type=jnp.float32),
        ("dp", "ctx"),
        scatter_dimension=0,
        tiled=True,
    )
    grad_act = jnp.einsum("rd,fd->rf", grad_top, down_b, preferred_element_type=jnp.float32)
    grad_gate = (
        grad_act * up_values * sigmoid_gate * (1.0 + gate_values * (1.0 - sigmoid_gate))
    ).astype(jnp.bfloat16)
    grad_up = (grad_act * gate_values * sigmoid_gate).astype(jnp.bfloat16)
    grad_gate_up = jnp.concatenate([grad_gate, grad_up], axis=1)
    left_part = hidden_two
    gate_up_share = lax.psum_scatter(
        jnp.einsum("rd,rf->df", left_part, grad_gate_up, preferred_element_type=jnp.float32),
        ("dp", "ctx"),
        scatter_dimension=0,
        tiled=True,
    )
    ff_width = gate_full.shape[1]
    gate_share = gate_up_share[:, :ff_width]
    up_share = gate_up_share[:, ff_width:]
    grad_hidden_two = jnp.einsum(
        "rf,df->rd", grad_gate, gate_b, preferred_element_type=jnp.float32
    ) + jnp.einsum("rf,df->rd", grad_up, up_b, preferred_element_type=jnp.float32)
    grad_middle_norm, grad_gain_two = normalize_back(
        grad_hidden_two, normed_two, inverse_two, gain_two_b
    )
    grad_middle = grad_top.astype(jnp.float32) + grad_middle_norm
    gain_one_b, qkv_b, bias_b, out_b = (
        lax.all_gather(gain_attn, "dp", axis=0, tiled=True),
        lax.all_gather(w_qkv, "dp", axis=0, tiled=True),
        lax.all_gather(b_qkv, "dp", axis=0, tiled=True),
        lax.all_gather(w_out, "dp", axis=0, tiled=True),
    )
    grad_branch = grad_middle.astype(jnp.bfloat16)
    grad_attn = jnp.einsum(
        "rd,qd->rq", grad_branch, out_b, preferred_element_type=jnp.float32
    ).astype(jnp.bfloat16)
    grad_heads = grad_attn.reshape(seq_count, tok_count, KV_HEADS, groups, HEAD_DIM).transpose(
        0, 2, 3, 1, 4
    )
    delta = jnp.sum(grad_heads.astype(jnp.float32) * attn_rows, axis=-1)
    zero_query = jnp.zeros((seq_count, KV_HEADS, groups, tok_count, HEAD_DIM), jnp.float32)
    zero_pair = jnp.zeros((2, seq_count, tok_count, KV_HEADS, HEAD_DIM), jnp.float32)

    def back_step(step_index, loop_carry):
        grad_query, pair_now, grad_pair = loop_carry
        source = (ctx_place - step_index) % ctx_count
        allowed = visible(source * tok_count + local_places)
        part_query, part_pair = attend_back(
            queries, pair_now, allowed, log_total, grad_heads, delta, score_scale
        )
        pair_now = from_behind(pair_now, "ctx", 1)
        grad_pair = from_behind((grad_pair + part_pair).astype(jnp.bfloat16), "ctx", 1).astype(
            jnp.float32
        )
        return (grad_query + part_query, pair_now, grad_pair)

    grad_query, pair_home, grad_pair = lax.fori_loop(
        0, ctx_count, back_step, (zero_query, kv_pair, zero_pair)
    )
    grad_query_rows = grad_query.transpose(0, 3, 1, 2, 4).reshape(row_count, HEADS, HEAD_DIM)
    grad_query_raw = unrotate(grad_query_rows, cosines, sines).reshape(row_count, query_width)
    grad_key_raw = unrotate(
        grad_pair[0].reshape(row_count, KV_HEADS, HEAD_DIM), cosines, sines
    ).reshape(row_count, kv_width)
    grad_proj = jnp.concatenate(
        [grad_query_raw, grad_key_raw, grad_pair[1].reshape(row_count, kv_width)], axis=1
    ).astype(jnp.bfloat16)
    grad_bias = jnp.sum(grad_proj.astype(jnp.float32), axis=0)
    grad_hidden_one = jnp.einsum("rc,dc->rd", grad_proj, qkv_b, preferred_element_type=jnp.float32)
    grad_input_norm, grad_gain_one = normalize_back(
        grad_hidden_one, normed_one, inverse_one, gain_one_b
    )
    grad_tokens = (grad_middle + grad_input_norm).reshape(seq_count, tok_count, width)
    attn_share = lax.psum_scatter(
        jnp.concatenate(
            [
                jnp.einsum("rd,rc->dc", hidden_one, grad_proj, preferred_element_type=jnp.float32),
                jnp.einsum("rq,rd->qd", attn_flat, grad_branch, preferred_element_type=jnp.float32),
            ],
            axis=1,
        ),
        ("dp", "ctx"),
        scatter_dimension=0,
        tiled=True,
    )
    qkv_share = attn_share[:, :proj_width]
    out_share = attn_share[:, proj_width:]
    gain_one_share, bias_share, gain_two_share = (
        lax.psum_scatter(grad_gain_one, ("dp", "ctx"), scatter_dimension=0, tiled=True),
        lax.psum_scatter(grad_bias, ("dp", "ctx"), scatter_dimension=0, tiled=True),
        lax.psum_scatter(grad_gain_two, ("dp", "ctx"), scatter_dimension=0, tiled=True),
    )
    return (
        block_out,
        grad_tokens,
        gain_one_share,
        qkv_share,
        bias_share,
        out_share,
        gain_two_share,
        gate_share,
        up_share,
        down_share,
    )


def solution(mesh):
    return jax.shard_map(
        body,
        mesh=mesh,
        in_specs=(
            P("dp", "ctx", None),
            P("dp", "ctx"),
            P(),
            P("dp", "ctx", None),
            P("dp"),
            P("dp", None),
            P("dp"),
            P("dp", None),
            P("dp"),
            P("dp", None),
            P("dp", None),
            P("dp", None),
        ),
        out_specs=(
            P("dp", "ctx", None),
            P("dp", "ctx", None),
            P(("dp", "ctx")),
            P(("dp", "ctx"), None),
            P(("dp", "ctx")),
            P(("dp", "ctx"), None),
            P(("dp", "ctx")),
            P(("dp", "ctx"), None),
            P(("dp", "ctx"), None),
            P(("dp", "ctx"), None),
        ),
        check_vma=False,
    )
```

profile of v0, /device:TPU:0, one launch (start us, length us, event | category | flops | bytes accessed | tf_op | source)
XLA Modules:
  0.0 2639.7 jit_solution(16025676978261663640)
XLA Ops:
  10.8 9.6 all-gather.2
  21.0 8.3 all-gather
  29.4 7.4 all-gather.1
  38.1 44.6 %all-gather.9.cloned.1.call-done = bf16[1536,2048]{1,0:T(8,128)(2,1)} async-done(((bf16[384,2048]{1,0:T(8,128)(2,1)}), bf16[1536,2048]{1,0:T(8,128)(2,1)}) %all-gather.9.cloned.1.call-update) | async-done | bytes 6291472 | tf_op jit(solution)/shard_map/all_gather | solution.py:161
  93.4 44.3 %while.44 = (s32[]{:T(128)}, f32[1,2,6,128]{3,2,1,0:T(8,128)S(1)}, f32[1,2,6,128]{3,2,1,0:T(8,128)S(1)}, f32[1,2,6,128,128]{4,3,2,1,0:T(8,128)S(1)}, bf16[2,1,12...) while((s32[]{:T(128)}, f32[1,2,6,128]{3,2,1,0:T(8,128)S(1)}, ...), condition=%wide.region_6.7_spmd.clone, body=%wide.region_2.6_spmd.clone.sunk | while | flops 102664848 | bytes 5382022 | solution.py:202
  147.1 243.3 %all-gather.15.cloned.1.call-done = bf16[1536,8960]{1,0:T(8,128)(2,1)} async-done(((bf16[384,8960]{1,0:T(8,128)(2,1)}), bf16[1536,8960]{1,0:T(8,128)(2,1)}) %all-gather.15.cloned.1.call-update) | async-done | bytes 27525136 | tf_op jit(solution)/shard_map/all_gather | solution.py:221
  390.5 15.8 fusion.96
  406.3 232.9 %all-gather.13.cloned.1.call-done = bf16[1536,8960]{1,0:T(8,128)(2,1)} async-done(((bf16[384,8960]{1,0:T(8,128)(2,1)}), bf16[1536,8960]{1,0:T(8,128)(2,1)}) %all-gather.13.cloned.1.call-update) | async-done | bytes 27525136 | tf_op jit(solution)/shard_map/all_gather | solution.py:220
  639.2 15.8 fusion.95
  655.0 232.9 %all-gather.17.cloned.1.call-done = bf16[8960,1536]{1,0:T(8,128)(2,1)} async-done(((bf16[2240,1536]{1,0:T(8,128)(2,1)}), bf16[8960,1536]{1,0:T(8,128)(2,1)}) %all-gather.17.cloned.1.call-update) | async-done | bytes 27525136 | tf_op jit(solution)/shard_map/all_gather | solution.py:222
  887.9 18.6 multiply_convert_fusion
  906.5 14.5 fusion.97
  921.1 16.0 multiply_reduce_fusion
  946.1 90.4 %while.45 = (s32[]{:T(128)}, f32[1,2,6,128,128]{4,3,2,1,0:T(8,128)S(1)}, bf16[2,1,128,2,128]{4,2,3,1,0:T(8,128)(2,1)}, f32[2,1,128,2,128]{4,2,3,1,0:T(8,128)S(1)...) while((s32[]{:T(128)}, ...), condition=%wide.region_15.16_spmd.clone, body=%wide.region_13.15_spmd.clone.sunk | while | flops 254207632 | bytes 9553853 | solution.py:298
  951.8 4.6 collective-permute-done.2
  961.5 6.2 collective-permute-done.2
  972.8 6.2 collective-permute-done.2
  984.1 6.2 collective-permute-done.2
  995.3 6.2 collective-permute-done.2
  1006.6 6.2 collective-permute-done.2
  1017.9 6.2 collective-permute-done.2
  1029.1 6.2 collective-permute-done.2
  1036.7 6.1 fusion.72
  1048.1 7.9 pad_maximum_fusion
  1056.9 50.7 %fusion.42 = f32[1536,17920]{1,0:T(8,128)} fusion(bf16[128,1536]{1,0:T(8,128)(2,1)S(1)} %copy-done.3, bf16[128,8960]{1,0:T(8,128)(2,1)} %get-tuple-element.822, bf16[128,8960]{1,0:T(8,128)(2,1)} %get-tuple-element.823), kind=kOutput, calls=%fused_computation.72 | convolution fusion | flops 7055605760 | bytes 115081216 | tf_op jit(solution)/shard_map/rd,rf->df/dot_general | solution.py:253
  1108.7 23.7 fusion.67
  1132.6 6.0 fusion.61
  1138.6 40.6 %all-reduce.4 = (f32[1536]{0:T(1024)S(1)}, f32[2048]{0:T(1024)S(1)}, f32[1536]{0:T(1024)S(1)}) all-reduce(f32[1536]{0:T(1024)S(1)} %get-tuple-element.771, f32[2048]{0:T(1024)S(1)} %convert_reduce_fusion, f32[1536]{0:T(1024)S(1)} %copy-done.18), channel_id=2, replica_groups=mesh['dp'=4,'ctx'=8] {'dp','ctx'}, use_global_device_ids=true, to_apply=%region_18.19.clone | all-reduce | flops 5120 | bytes 40960
  1183.3 15.0 fusion.47
  1198.2 81.3 %reduce-scatter.6.cloned.1.call-done = f32[48,3584]{1,0:T(8,128)} async-done(((f32[1536,3584]{1,0:T(8,128)}), f32[48,3584]{1,0:T(8,128)}) %reduce-scatter.6.cloned.1.call-update) | async-done | bytes 688144 | tf_op jit(solution)/shard_map/reduce_scatter | solution.py:315
  1283.0 883.4 %reduce-scatter.8.cloned.1.call-done = f32[48,17920]{1,0:T(8,128)} async-done(((f32[1536,17920]{1,0:T(8,128)}), f32[48,17920]{1,0:T(8,128)}) %reduce-scatter.8.cloned.1.call-update) | async-done | bytes 3440656 | tf_op jit(solution)/shard_map/reduce_scatter | solution.py:252
  2170.4 462.2 %reduce-scatter.10.cloned.1.call-done = f32[280,1536]{1,0:T(8,128)} async-done(((f32[8960,1536]{1,0:T(8,128)}), f32[280,1536]{1,0:T(8,128)}) %reduce-scatter.10.cloned.1.call-update) | async-done | bytes 1720336
  (361 shorter events, 138.2 us)
Async XLA Ops:
  7.2 75.5 %all-gather.9.cloned.1.call-start = ((), (), s32[]{:S(2)}) async-start(), calls=%async_computation.3 | async-start | bytes 7864320 | tf_op jit(solution)/shard_map/all_gather | solution.py:161
  7.9 135.7 %all-gather.11.cloned.1.call-start = ((), (), s32[]{:S(2)}) async-start(), calls=%async_computation.4 | async-start | bytes 5898240 | tf_op jit(solution)/shard_map/all_gather | solution.py:163
  8.7 381.8 %all-gather.15.cloned.1.call-start = ((), (), s32[]{:S(2)}) async-start(), calls=%async_computation.6 | async-start | bytes 34406400 | tf_op jit(solution)/shard_map/all_gather | solution.py:221
  9.4 629.8 %all-gather.13.cloned.1.call-start = ((), (), s32[]{:S(2)}) async-start(), calls=%async_computation.5 | async-start | bytes 34406400 | tf_op jit(solution)/shard_map/all_gather | solution.py:220
  10.0 877.9 %all-gather.17.cloned.1.call-start = ((), (), s32[]{:S(2)}) async-start(), calls=%async_computation.7 | async-start | bytes 34406400 | tf_op jit(solution)/shard_map/all_gather | solution.py:222
  10.6 1269.0 %reduce-scatter.6.cloned.1.call-start = ((), (), s32[]{:S(2)}) async-start(), calls=%async_computation.8 | async-start | bytes 22708224 | tf_op jit(solution)/shard_map/reduce_scatter | solution.py:315
  94.0 6.2 collective-permute-start
  100.3 6.2 collective-permute-start
  106.5 6.2 collective-permute-start
  112.8 6.2 collective-permute-start
  119.0 6.2 collective-permute-start
  125.3 6.2 collective-permute-start
  131.5 6.2 collective-permute-start
  147.1 492.1 %copy-start.2 = (bf16[128,1536]{1,0:T(8,128)(2,1)}, bf16[128,1536]{1,0:T(8,128)(2,1)S(1)}, u32[]{:S(2)}) copy-start(bf16[128,1536]{1,0:T(8,128)(2,1)S(1)} %multiply_convert_fusion.3) | copy-start | bytes 1179652
  947.0 10.3 collective-permute-start.1
  949.9 6.5 collective-permute-start.2
  958.3 10.3 collective-permute-start.1
  961.2 6.5 collective-permute-start.2
  969.6 10.3 collective-permute-start.1
  972.5 6.5 collective-permute-start.2
  980.8 10.3 collective-permute-start.1
  983.7 6.5 collective-permute-start.2
  992.1 10.3 collective-permute-start.1
  995.0 6.5 collective-permute-start.2
  1003.4 10.3 collective-permute-start.1
  1006.3 6.5 collective-permute-start.2
  1014.6 10.3 collective-permute-start.1
  1017.5 6.5 collective-permute-start.2
  1025.9 10.3 collective-permute-start.1
  1028.8 6.5 collective-permute-start.2
  1056.0 1110.5 %reduce-scatter.8.cloned.1.call-start = ((), (), s32[]{:S(2)}) async-start(), calls=%async_computation.9 | async-start | bytes 113541120 | tf_op jit(solution)/shard_map/reduce_scatter | solution.py:252
  1107.7 1524.9 %reduce-scatter.10.cloned.1.call-start = ((), (), s32[]{:S(2)}) async-start(), calls=%async_computation.10 | async-start | bytes 56770560
  (29 other events, 1204.8 us)
Sparse Core Ops, SparseCore 0:
  9.8 72.8 all-gather.8
  84.6 56.9 all-gather.10
  143.4 247.0 all-gather.14
  392.2 246.9 all-gather.12
  640.9 246.9 all-gather.16
  1056.1 223.4 reduce-scatter.5
  1286.0 880.3 reduce-scatter.7
  2173.4 459.1 reduce-scatter.9
where the time goes:
time: 2640 us
  waiting for transfers between devices  2260 us (86%)
  matrix products  223 us (8%)
  blocking collectives  65.9 us (2%)
  other arithmetic  40.8 us (2%)
  local copies, waits for them, and re-layouts  28.8 us (1%)
    reduce_scatter x1, waiting for transfers between devices, body(): lax.psum_scatter(jnp.einsum('rd,rf->df', left_part, grad_gate_up, preferr...  883 us
    unnamed x9, waiting for transfers between devices  465 us
    all_gather x1, waiting for transfers between devices, body(): lax.all_gather(w_up, 'dp', axis=0, tiled=True)  243 us
    all_gather x1, waiting for transfers between devices, body(): lax.all_gather(w_gate, 'dp', axis=0, tiled=True)  233 us
    all_gather x1, waiting for transfers between devices, body(): lax.all_gather(w_down, 'dp', axis=0, tiled=True)  233 us
    reduce_scatter x1, waiting for transfers between devices, body(): lax.psum_scatter(jnp.concatenate([jnp.einsum('rd,rc->dc', hidden_one, gra...  81.3 us
    ppermute x23, waiting for transfers between devices, from_behind(): return lax.ppermute(value, axis, pairs)  77.9 us
  transfers between devices with their start and end apart: 31, of which 22 were waited for; matrix products, arithmetic and copies ran while one was open for 8% of the time, Pallas kernels for 0%

commit v1 on v0

v1 whole, which is shorter than its diff:
```python
import functools
import math

import jax
import jax.numpy as jnp
from jax import lax
from jax.experimental import pallas as pl
from jax.experimental.pallas import tpu as pltpu
from jax.sharding import PartitionSpec as P

HEADS = 12
KV_HEADS = 2
HEAD_DIM = 128
GROUPS = HEADS // KV_HEADS
QW = HEADS * HEAD_DIM
KW = KV_HEADS * HEAD_DIM
STEP_HEADS = 3

rope_base = 1000000.0
norm_eps = 1e-06
masked_score = -1e30
score_scale = 1.0 / math.sqrt(HEAD_DIM)
f32 = jnp.float32
bf16 = jnp.bfloat16


def exchange(value, axis, bit):
    count = lax.axis_size(axis)
    return lax.ppermute(value, axis, [(i, i ^ bit) for i in range(count)])


def mm(left, right, dims, out=f32):
    return lax.dot_general(left, right, (dims, ((), ())), preferred_element_type=out)


def gather_pieces(shard):
    rows = shard.shape[0]
    half = rows // 2
    from_x = exchange(shard, "dp", 1)
    from_y = exchange(shard, "dp", 2)
    far_low = exchange(from_x[:half], "dp", 2)
    far_high = exchange(from_y[half:], "dp", 1)
    return [(0, 0, shard), (1, 0, from_x), (2, 0, from_y), (3, 0, far_low), (3, half, far_high)]


def gather_rows(shard, place):
    count = lax.axis_size("dp")
    if count != 4:
        return lax.all_gather(shard, "dp", axis=0, tiled=True)
    rows = shard.shape[0]
    full = jnp.zeros((count * rows, shard.shape[1]), shard.dtype)
    for rel, offset, block in gather_pieces(shard):
        full = lax.dynamic_update_slice(full, block, ((place ^ rel) * rows + offset, 0))
    return full


def gather_rows_shared(shard, place, core):
    count = lax.axis_size("dp")
    if count != 4:
        return lax.all_gather(shard, "dp", axis=0, tiled=True)
    rows, cols = shard.shape
    part = rows // 2
    mine = lax.dynamic_slice(shard, (core * part, 0), (part, cols))
    full = jnp.zeros((count * rows, cols), shard.dtype)
    full = lax.dynamic_update_slice(full, shard, (place * rows, 0))
    for rel, offset, block in gather_pieces(mine)[1:]:
        base = (place ^ rel) * rows + offset
        full = lax.dynamic_update_slice(full, block, (base + core * part, 0))
        full = lax.dynamic_update_slice(
            full, exchange(block, "ctx", 1), (base + (1 - core) * part, 0)
        )
    return full


def scatter_blocks(block_of):
    far = block_of(3, bf16)
    half = far.shape[0] // 2
    low_in = exchange(far[:half], "dp", 1)
    high_in = exchange(far[half:], "dp", 2)
    x_block = block_of(1, f32)
    y_block = block_of(2, f32)
    x_out = jnp.concatenate(
        [x_block[:half].astype(bf16), (x_block[half:] + high_in.astype(f32)).astype(bf16)]
    )
    y_out = jnp.concatenate(
        [(y_block[:half] + low_in.astype(f32)).astype(bf16), y_block[half:].astype(bf16)]
    )
    x_in = exchange(x_out, "dp", 1)
    y_in = exchange(y_out, "dp", 2)
    return block_of(0, f32) + (x_in.astype(f32) + y_in.astype(f32))


def rope_rows(u, cosines, sines):
    return u * cosines + pltpu.roll(u, HEAD_DIM // 2, 1) * sines


def unrope_rows(w, cosines, sines):
    return w * cosines - pltpu.roll(w, HEAD_DIM // 2, 1) * sines


NT = ((1,), (1,))
NN = ((1,), (0,))
TN = ((0,), (0,))


def attend_kernel(q_ref, kv_ref, qcos, qsin, kcos, ksin, qidx, kidx, o_ref, lse_ref, qr_ref, kr_ref, v_ref):
    rows = q_ref.shape[0]
    for g in range(KV_HEADS):
        cols = pl.ds(g * HEAD_DIM, HEAD_DIM)
        kr_ref[:, cols] = rope_rows(kv_ref[:, cols], kcos[...], ksin[...]).astype(bf16)
        v_ref[:, cols] = kv_ref[:, pl.ds(KW + g * HEAD_DIM, HEAD_DIM)].astype(bf16)
    for h in range(HEADS):
        cols = pl.ds(h * HEAD_DIM, HEAD_DIM)
        qr_ref[:, cols] = rope_rows(q_ref[:, cols], qcos[...], qsin[...]).astype(bf16)
    lane = lax.broadcasted_iota(jnp.int32, (rows, HEAD_DIM), 1)
    lse_ref[...] = jnp.zeros_like(lse_ref)

    def step(i, carry):
        g = i * STEP_HEADS // GROUPS
        kcols = pl.ds(pl.multiple_of(g * HEAD_DIM, HEAD_DIM), HEAD_DIM)
        k = kr_ref[:, kcols]
        v = v_ref[:, kcols]
        allowed = kidx[...] <= qidx[...]
        for j in range(STEP_HEADS):
            h = i * STEP_HEADS + j
            cols = pl.ds(pl.multiple_of(h * HEAD_DIM, HEAD_DIM), HEAD_DIM)
            s = mm(qr_ref[:, cols], k, NT) * score_scale
            s = jnp.where(allowed, s, masked_score)
            top = jnp.max(s, axis=-1, keepdims=True)
            e = jnp.exp(s - top)
            total = jnp.sum(e, axis=-1, keepdims=True)
            o = mm(e.astype(bf16), v, NN) / total
            o_ref[:, cols] = o.astype(bf16)
            lse_ref[...] = jnp.where(lane == h, top + jnp.log(total), lse_ref[...])
        return carry

    lax.fori_loop(0, HEADS // STEP_HEADS, step, 0)


def attend_back_kernel(q_ref, k_ref, v_ref, do_ref, lse_ref, qcos, qsin, qidx, kidx, dq_ref, dk_ref, dv_ref):
    rows = q_ref.shape[0]
    lane = lax.broadcasted_iota(jnp.int32, (rows, HEAD_DIM), 1)
    dk_ref[...] = jnp.zeros_like(dk_ref)
    dv_ref[...] = jnp.zeros_like(dv_ref)

    def step(i, carry):
        g = i * STEP_HEADS // GROUPS
        kcols = pl.ds(pl.multiple_of(g * HEAD_DIM, HEAD_DIM), HEAD_DIM)
        k = k_ref[:, kcols]
        v = v_ref[:, kcols]
        allowed = kidx[...] <= qidx[...]
        dk = dk_ref[:, kcols]
        dv = dv_ref[:, kcols]
        for j in range(STEP_HEADS):
            h = i * STEP_HEADS + j
            cols = pl.ds(pl.multiple_of(h * HEAD_DIM, HEAD_DIM), HEAD_DIM)
            q = q_ref[:, cols]
            do = do_ref[:, cols]
            lse = jnp.sum(jnp.where(lane == h, lse_ref[...], 0.0), axis=-1, keepdims=True)
            s = mm(q, k, NT) * score_scale
            p = jnp.where(allowed, jnp.exp(s - lse), 0.0)
            dp = mm(do, v, NT)
            delta = jnp.sum(p * dp, axis=-1, keepdims=True)
            ds = (p * (dp - delta)).astype(bf16)
            dq = mm(ds, k, NN) * score_scale
            dq_ref[:, cols] = unrope_rows(dq, qcos[...], qsin[...]).astype(bf16)
            dk = dk + mm(ds, q, TN) * score_scale
            dv = dv + mm(p.astype(bf16), do, TN)
        dk_ref[:, kcols] = dk
        dv_ref[:, kcols] = dv
        return carry

    lax.fori_loop(0, HEADS // STEP_HEADS, step, 0)


def whole(count):
    return [pl.BlockSpec(memory_space=pltpu.VMEM)] * count


def attend(q_raw, kv_raw, tables_q, tables_k, qidx, kidx):
    rows, keys = q_raw.shape[0], kv_raw.shape[0]
    shape = jax.ShapeDtypeStruct
    return pl.pallas_call(
        attend_kernel,
        out_shape=(
            shape((rows, QW), bf16),
            shape((rows, HEAD_DIM), f32),
            shape((rows, QW), bf16),
            shape((keys, KW), bf16),
            shape((keys, KW), bf16),
        ),
        in_specs=whole(8),
        out_specs=tuple(whole(5)),
        cost_estimate=pl.CostEstimate(
            flops=4 * rows * keys * QW, bytes_accessed=8 * keys * KW, transcendentals=rows * keys * HEADS
        ),
        name="attend",
    )(q_raw, kv_raw, *tables_q, *tables_k, qidx, kidx)


def attend_back(q, k, v, do, lse, tables_q, qidx, kidx):
    rows, keys = q.shape[0], k.shape[0]
    shape = jax.ShapeDtypeStruct
    return pl.pallas_call(
        attend_back_kernel,
        out_shape=(shape((rows, QW), bf16), shape((keys, KW), f32), shape((keys, KW), f32)),
        in_specs=whole(9),
        out_specs=tuple(whole(3)),
        cost_estimate=pl.CostEstimate(
            flops=10 * rows * keys * QW, bytes_accessed=16 * keys * KW, transcendentals=rows * keys * HEADS
        ),
        name="attend_back",
    )(q, k, v, do, lse, *tables_q, qidx, kidx)


def rope_tables(positions):
    half = HEAD_DIM // 2
    steps = jnp.arange(half, dtype=f32)
    frequency = jnp.exp(-math.log(rope_base) * (2.0 * steps / HEAD_DIM))
    angles = positions.astype(f32)[:, None] * frequency[None, :]
    c, s = jnp.cos(angles), jnp.sin(angles)
    return jnp.concatenate([c, c], axis=-1), jnp.concatenate([-s, s], axis=-1)


def unrope(w, cosines, sines):
    heads = w.reshape(w.shape[0], -1, HEAD_DIM)
    rolled = jnp.roll(heads, HEAD_DIM // 2, axis=-1)
    return (heads * cosines[:, None, :] - rolled * sines[:, None, :]).reshape(w.shape)


def inv_rms(rows):
    return lax.rsqrt(jnp.mean(rows * rows, axis=-1, keepdims=True) + norm_eps)


def norm_back(grad_out, normed, inverse, gain):
    scaled = grad_out * gain
    return inverse * (scaled - normed * jnp.mean(scaled * normed, axis=-1, keepdims=True))


def body(
    tokens, positions, block_order, cotangent, gain_attn, w_qkv, b_qkv, w_out, gain_mlp, w_gate, w_up, w_down
):
    _, rows, width = tokens.shape
    n_dp, n_ctx = lax.axis_size("dp"), lax.axis_size("ctx")
    place, ctx = lax.axis_index("dp"), lax.axis_index("ctx")
    core = ctx % 2
    n_all = n_dp * n_ctx
    length = rows * n_ctx
    ff = w_gate.shape[1]
    chunk = ff // n_all
    sub = rows // 2
    proj = QW + 2 * KW

    small = jnp.concatenate([gain_attn, gain_mlp, b_qkv])[None]
    small = lax.all_gather(small, "dp", axis=0, tiled=True)
    d_loc = gain_attn.shape[0]
    gain_one = small[:, :d_loc].reshape(1, width).astype(f32)
    gain_two = small[:, d_loc : 2 * d_loc].reshape(1, width).astype(f32)
    bias = small[:, 2 * d_loc :].reshape(1, proj).astype(f32)

    qkv_full = gather_rows_shared(w_qkv, place, core)
    out_full = gather_rows_shared(w_out, place, core)

    def ff_columns(w):
        return jnp.concatenate(
            [lax.dynamic_slice(w, (0, (d * n_ctx + ctx) * chunk), (w.shape[0], chunk)) for d in range(n_dp)],
            axis=1,
        )

    down = gather_rows(lax.dynamic_slice(w_down, (ctx * chunk, 0), (chunk, width)), place)
    gate = gather_rows(ff_columns(w_gate), place)
    up = gather_rows(ff_columns(w_up), place)

    places = jnp.arange(length, dtype=jnp.int32)
    index = jnp.repeat(block_order, sub) * sub + places % sub
    own_index = lax.dynamic_slice(index, (ctx * rows,), (rows,))
    offset = positions[0, 0] - own_index[0]
    tables_k = rope_tables(index + offset)
    tables_q = tuple(lax.dynamic_slice(t, (ctx * rows, 0), (rows, HEAD_DIM)) for t in tables_k)
    qidx, kidx = own_index[:, None], index[None, :]

    x_full = lax.all_gather(tokens[0], "ctx", axis=0, tiled=True)
    dy_full = lax.all_gather(cotangent[0], "ctx", axis=0, tiled=True)
    x_all = x_full.astype(f32)
    h1_full = (x_all * inv_rms(x_all) * gain_one).astype(bf16)
    x = tokens[0].astype(f32)
    inv1 = inv_rms(x)
    n1 = x * inv1
    h1 = (n1 * gain_one).astype(bf16)
    q_raw = mm(h1, qkv_full[:, :QW], NN) + bias[:, :QW]
    kv_raw = mm(h1_full, qkv_full[:, QW:], NN) + bias[:, QW:]
    ob, lse, q_rot, k_rot, v_rows = attend(q_raw, kv_raw, tables_q, tables_k, qidx, kidx)
    ob_full = lax.all_gather(ob, "ctx", axis=0, tiled=True)
    r1_all = x_all + mm(ob_full, out_full, NN)
    h2_full = (r1_all * inv_rms(r1_all) * gain_two).astype(bf16)
    r1 = lax.dynamic_slice(r1_all, (ctx * rows, 0), (rows, width))
    inv2 = inv_rms(r1)
    n2 = r1 * inv2

    g = mm(h2_full, gate, NN)
    u = mm(h2_full, up, NN)
    sig = jax.nn.sigmoid(g)
    act = (g * sig * u).astype(bf16)
    da = mm(dy_full, down, NT)
    dgate = (da * u * sig * (1.0 + g * (1.0 - sig))).astype(bf16)
    dup = (da * g * sig).astype(bf16)
    dh2_part = (mm(dgate, gate, NT) + mm(dup, up, NT)).astype(bf16)
    dh2 = lax.psum_scatter(dh2_part, "ctx", scatter_dimension=0, tiled=True).astype(f32)
    mlp_part = mm(act, down, NN).astype(bf16)
    mlp = lax.psum_scatter(mlp_part, "ctx", scatter_dimension=0, tiled=True).astype(f32)
    block_out = (r1 + mlp).astype(bf16)[None]

    if n_dp == 4:
        grad_down_all = mm(act, dy_full, TN)

        def down_block(rel, dtype):
            start = (place ^ rel) * chunk
            return lax.dynamic_slice(grad_down_all, (start, 0), (chunk, width)).astype(dtype)

        grad_down = scatter_blocks(down_block)

        def rows_block(grad):
            def block(rel, dtype):
                cols = lax.dynamic_slice(h2_full, (0, (place ^ rel) * d_loc), (length, d_loc))
                return mm(cols, grad, TN, f32).astype(dtype)

            return scatter_blocks(block).astype(bf16)

        gate_rows = rows_block(dgate)
        up_rows = rows_block(dup)
    else:
        scatter = functools.partial(lax.psum_scatter, axis_name="dp", scatter_dimension=0, tiled=True)
        grad_down = scatter(mm(act, dy_full, TN).astype(bf16)).astype(f32)
        gate_rows = scatter(mm(h2_full, dgate, TN).astype(bf16))
        up_rows = scatter(mm(h2_full, dup, TN).astype(bf16))
    own_rows = d_loc // n_ctx
    both = jnp.stack([gate_rows, up_rows]).reshape(2, n_ctx, own_rows, n_dp * chunk).transpose(1, 0, 2, 3)
    both = lax.all_to_all(both, "ctx", 0, 0, tiled=True)

    def natural(part):
        cols = part.reshape(n_ctx, own_rows, n_dp, chunk).transpose(1, 2, 0, 3)
        return cols.reshape(own_rows, ff).astype(f32)

    grad_gate, grad_up = natural(both[:, 0]), natural(both[:, 1])

    grad_gain_two = jnp.sum(dh2 * n2, axis=0)
    dr1 = cotangent[0].astype(f32) + norm_back(dh2, n2, inv2, gain_two)
    dattn = dr1.astype(bf16)
    do = mm(dattn, out_full, NT).astype(bf16)
    dq, dk_part, dv_part = attend_back(q_rot, k_rot, v_rows, do, lse, tables_q, qidx, kidx)
    dkv_part = jnp.concatenate([dk_part, dv_part], axis=1).astype(bf16)
    dkv = lax.psum_scatter(dkv_part, "ctx", scatter_dimension=0, tiled=True).astype(f32)
    dk = unrope(dkv[:, :KW], *tables_q)
    dqkv = jnp.concatenate([dq, dk.astype(bf16), dkv[:, KW:].astype(bf16)], axis=1)
    dh1 = mm(dqkv, qkv_full, NT)
    grad_gain_one = jnp.sum(dh1 * n1, axis=0)
    grad_tokens = (dr1 + norm_back(dh1, n1, inv1, gain_one))[None]
    grad_bias = jnp.sum(dqkv.astype(f32), axis=0)

    def columns(v):
        cols = v.shape[1] // n_ctx
        return lax.all_to_all(v.reshape(rows, n_ctx, cols).transpose(1, 0, 2), "ctx", 0, 0, tiled=True).reshape(length, cols)

    grad_qkv_cols = mm(h1_full, columns(dqkv), TN)
    grad_out_cols = mm(ob_full, columns(dattn), TN)
    cols_qkv, cols_out = proj // n_ctx, width // n_ctx
    share = jnp.concatenate([grad_qkv_cols, grad_out_cols], axis=1).astype(bf16)
    share = share.reshape(n_all, width // n_all, cols_qkv + cols_out)
    share = lax.all_to_all(share, ("dp", "ctx"), 0, 0, tiled=True)
    share = jnp.sum(share.reshape(n_dp, n_ctx, width // n_all, -1).astype(f32), axis=0).transpose(1, 0, 2)
    grad_qkv = share[:, :, :cols_qkv].reshape(width // n_all, proj)
    grad_out = share[:, :, cols_qkv:].reshape(width // n_all, width)
    gain_width = width // n_all
    vectors = jnp.concatenate(
        [grad_gain_one.reshape(n_all, -1), grad_gain_two.reshape(n_all, -1), grad_bias.reshape(n_all, -1)], axis=1
    )
    vectors = jnp.sum(lax.all_to_all(vectors, ("dp", "ctx"), 0, 0, tiled=True), axis=0)
    return (
        block_out,
        grad_tokens,
        vectors[:gain_width],
        grad_qkv,
        vectors[2 * gain_width :],
        grad_out,
        vectors[gain_width : 2 * gain_width],
        grad_gate,
        grad_up,
        grad_down,
    )


def solution(mesh):
    rows = P(("dp", "ctx"), None)
    vector = P(("dp", "ctx"))
    return jax.shard_map(
        body,
        mesh=mesh,
        in_specs=(
            P("dp", "ctx", None),
            P("dp", "ctx"),
            P(),
            P("dp", "ctx", None),
            P("dp"),
            P("dp", None),
            P("dp"),
            P("dp", None),
            P("dp"),
            P("dp", None),
            P("dp", None),
            P("dp", None),
        ),
        out_specs=(
            P("dp", "ctx", None),
            P("dp", "ctx", None),
            vector,
            rows,
            vector,
            rows,
            vector,
            rows,
            rows,
            rows,
        ),
        check_vma=False,
    )
```

time: 2640 us -> 629 us (0.24)
  waiting for transfers between devices: 2260 us -> 76.3 us
  local copies, waits for them, and re-layouts: 28.8 us -> 226 us
  matrix products: 223 us -> 125 us
  starting transfers between devices: 2.35 us -> 58.6 us
  blocking collectives: 65.9 us -> 28.4 us
  other arithmetic: 40.8 us -> 71.5 us
    reduce_scatter x2 -> x3, waiting for transfers between devices: 965 us -> 17 us  [the longest x1 17 us: body(): lax.psum_scatter(dh2_part, 'ctx', scatter_dimension=0, tiled=True)]
    all_gather x5 -> x3, waiting for transfers between devices: 754 us -> 0.01 us  [the longest x1 0.01 us: body(): x_full = lax.all_gather(tokens[0], 'ctx', axis=0, tiled=True)]
    unnamed x9 -> x6, waiting for transfers between devices: 465 us -> 0.76 us
    dot_general x70 -> x22, matrix products: 223 us -> 125 us  [mm(): lax.dot_general(left, right, (dims, ((), ())), preferred_element_type=out)]
    dynamic_update_slice x0 -> x31, local copies, waits for them, and re-layouts: none -> 73.9 us  [the longest x13 48.8 us: gather_rows(): lax.dynamic_update_slice(full, block, ((place ^ rel) * rows + offset, 0))]
    ppermute x23 -> x40, waiting for transfers between devices: 77.9 us -> 25.9 us  [exchange(): return lax.ppermute(value, axis, [(i, i ^ bit) for i in range(count)])]
    unnamed x1 -> x0, blocking collectives: 40.6 us -> none
    slice x8 -> x32, local copies, waits for them, and re-layouts: 8.65 us -> 47.8 us  [the longest x7 12.7 us: gather_pieces(): far_high = exchange(from_y[half:], 'dp', 1)]
  transfers between devices with their start and end apart: 31 -> 51, of which waited for: 22 -> 11; matrix products, arithmetic and copies ran while one was open for 8% -> 58% of each run, Pallas kernels for 0% -> 3%
where the time goes in v1:
time: 629 us; the launch traced here: 620 us
  local copies, waits for them, and re-layouts  226 us (36%)
  matrix products  125 us (20%)
  waiting for transfers between devices  76.3 us (12%)
  other arithmetic  71.5 us (11%)
  starting transfers between devices  58.6 us (9%)
  blocking collectives  28.4 us (5%)
  Pallas kernels  19.4 us (3%)
  between operations  15.3 us (2%)
    dot_general x22, matrix products, mm(): lax.dot_general(left, right, (dims, ((), ())), preferred_element_type=out)  125 us
    dynamic_update_slice x13, local copies, waits for them, and re-layouts, gather_rows(): lax.dynamic_update_slice(full, block, ((place ^ rel) * rows + offset, 0))  48.8 us
    ppermute x40, starting transfers between devices, exchange(): return lax.ppermute(value, axis, [(i, i ^ bit) for i in range(count)])  38.8 us
    all_gather x1, blocking collectives, body(): small = lax.all_gather(small, 'dp', axis=0, tiled=True)  28.4 us
    ppermute x40, waiting for transfers between devices, exchange(): return lax.ppermute(value, axis, [(i, i ^ bit) for i in range(count)])  25.9 us
    unnamed x118, local copies, waits for them, and re-layouts  21.4 us
    convert_element_type x6, local copies, waits for them, and re-layouts, natural(): return cols.reshape(own_rows, ff).astype(f32)  18.2 us
    reduce_scatter x1, waiting for transfers between devices, body(): lax.psum_scatter(dh2_part, 'ctx', scatter_dimension=0, tiled=True)  17 us
  transfers between devices with their start and end apart: 51, of which 11 were waited for; matrix products, arithmetic and copies ran while one was open for 58% of the time, Pallas kernels for 3%

profile of v1, /device:TPU:0, one launch (start us, length us, event | category | flops | bytes accessed | tf_op | source)
XLA Modules:
  0.0 620.5 jit_solution(11488675288117726115)
XLA Ops:
  18.6 28.4 %all-gather.3 = bf16[4,1,1280]{2,1,0:T(2,128)(2,1)S(1)} all-gather(bf16[1,1,1280]{2,1,0:T(2,128)(2,1)S(1)} %reshape.243), channel_id=3, replica_groups=mesh['dp'=4,'ctx'=8] {'dp'}, dimensions={0}, use_global_device_ids=true | all-gather | bytes 12800 | tf_op jit(solution)/shard_map/all_gather | solution.py:255
  51.5 4.5 constant_dynamic-slice_fusion.4
  93.7 4.6 fusion.19.kv_ref
  98.4 8.7 %attend.1 = (bf16[128,1536]{1,0:T(8,128)(2,1)}, f32[128,128]{1,0:T(8,128)}, bf16[128,1536]{1,0:T(8,128)(2,1)}, bf16[1024,256]{1,0:T(8,128)(2,1)}, bf16[1024,256]{1,0:T(8,128)(2,1)}) custom-call(f32[128,1536]{1,0:T(8,128)} %fusion.14.q_ref, f32[1024,512]{1,0:T(8,128)} %fusion.19.kv_ref, f32[128,128]{1,0:T(8,128)} %get-tuple-element.78.qcos, ...), custom_call_target="tpu_custom_call" | custom-call | flops 805306368 | bytes 2097152 | tf_op jit(solution)/shard_map/attend/pallas_call | solution.py:183
  144.2 7.4 %collective-permute-done.20 = bf16[384,1120]{0,1:T(8,128)(2,1)} collective-permute-done((bf16[384,1120]{0,1:T(8,128)(2,1)}, bf16[384,1120]{0,1:T(8,128)(2,1)}, u32[]{:S(2)}, u32[]{:S(2)}) %collective-permute-start.20) | collective-permute-done | bytes 860192 | tf_op jit(solution)/shard_map/ppermute | solution.py:29
  158.3 11.6 %collective-permute-done.24 = bf16[280,1536]{1,0:T(8,128)(2,1)S(1)} collective-permute-done((bf16[280,1536]{1,0:T(8,128)(2,1)}, bf16[280,1536]{1,0:T(8,128)(2,1)S(1)}, u32[]{:S(2)}, u32[]{:S(2)}) %collective-permute-start.24) | collective-permute-done | bytes 860192 | tf_op jit(solution)/shard_map/ppermute | solution.py:29
  216.3 6.7 %dynamic_update_slice.120 = bf16[1536,1120]{0,1:T(8,128)(2,1)} dynamic-update-slice(bf16[1536,1120]{0,1:T(8,128)(2,1)} %constant_dynamic-update-slice_fusion.6, bf16[192,1120]{0,1:T(8,128)(2,1)} %copy.105, s32[]{:T(128)S(6)} %select_n.156, s32[]{:T(128)} %constant.83.clone.1) | dynamic-update-slice | bytes 860164 | tf_op jit(solution)/shard_map/dynamic_update_slice | solution.py:53
  225.1 6.7 %dynamic_update_slice.125 = bf16[1536,1120]{0,1:T(8,128)(2,1)} dynamic-update-slice(bf16[1536,1120]{0,1:T(8,128)(2,1)} %constant_dynamic-update-slice_fusion.3, bf16[192,1120]{0,1:T(8,128)(2,1)} %copy.113, s32[]{:T(128)S(6)} %select_n.156, s32[]{:T(128)} %constant.83.clone.1) | dynamic-update-slice | bytes 860164 | tf_op jit(solution)/shard_map/dynamic_update_slice | solution.py:53
  233.9 7.0 %dynamic_update_slice.121 = bf16[1536,1120]{0,1:T(8,128)(2,1)} dynamic-update-slice(bf16[1536,1120]{0,1:T(8,128)(2,1)} %dynamic_update_slice.120, bf16[192,1120]{0,1:T(8,128)(2,1)} %copy.107, s32[]{:T(128)S(6)} %select_n.157, s32[]{:T(128)} %constant.83.clone.1) | dynamic-update-slice | bytes 860164 | tf_op jit(solution)/shard_map/dynamic_update_slice | solution.py:53
  243.0 7.1 %dynamic_update_slice.126 = bf16[1536,1120]{0,1:T(8,128)(2,1)} dynamic-update-slice(bf16[1536,1120]{0,1:T(8,128)(2,1)} %dynamic_update_slice.125, bf16[192,1120]{0,1:T(8,128)(2,1)} %copy.115, s32[]{:T(128)S(6)} %select_n.157, s32[]{:T(128)} %constant.83.clone.1) | dynamic-update-slice | bytes 860164 | tf_op jit(solution)/shard_map/dynamic_update_slice | solution.py:53
  256.5 8.8 %fusion.12 = f32[1120,1024]{1,0:T(8,128)} fusion(bf16[1120,1536]{1,0:T(8,128)(2,1)} %dynamic_update_slice.131, bf16[1,1024,1536]{2,1,0:T(8,128)(2,1)} %all-gather.12.cloned.1.call-done), kind=kOutput, calls=%fused_computation.24 | convolution fusion | flops 3523215360 | bytes 11173888 | tf_op jit(solution)/shard_map/dot_general | solution.py:33
  265.3 8.4 %multiply_reduce_fusion = (f32[1024]{0:T(1024)S(1)}, f32[1024,1536]{1,0:T(8,128)S(1)}) fusion(bf16[1024,1536]{1,0:T(8,128)(2,1)} %all-gather.8.cloned.1.call-done, bf16[1536,1536]{1,0:T(8,128)(2,1)} %constant_dynamic-update-slice_fusion.9, bf16[1,1024,1536]{2,1,0:T(8,128)(2,1)S(1)} %copy-done.1), kind=kOutput, calls=%fused_computation.8 | convolution fusion | flops 4838128640 | bytes 17305600 | tf_op jit(solution)/shard_map/dot_general | solution.py:33
  277.0 7.3 %fusion.90 = f32[1024,1120]{0,1:T(8,128)S(1)} fusion(bf16[1024,1536]{1,0:T(8,128)(2,1)S(1)} %multiply_convert_fusion, bf16[1536,1120]{0,1:T(8,128)(2,1)} %dynamic_update_slice.121), kind=kOutput, calls=%fused_computation.209 | convolution fusion | flops 3523215360 | bytes 11173888 | tf_op jit(solution)/shard_map/dot_general | solution.py:33
  284.3 20.5 %fusion.7 = (bf16[1024,1120]{0,1:T(8,128)(2,1)S(1)}, bf16[1024,1120]{0,1:T(8,128)(2,1)S(1)}, bf16[1024,1120]{0,1:T(8,128)(2,1)}) fusion(f32[1120,1024]{1,0:T(8,128)S(1)} %bitcast.164, f32[1024,1120]{0,1:T(8,128)S(1)} %fusion.90, bf16[1024,1536]{1,0:T(8,128)(2,1)S(1)} %multiply_convert_fusion, bf16[1536,1120]{0,1:T(8,128)(2,1)} %dynamic_update_slice.126), kind=kOutput, calls=%fused_computation.15 | convolution fusion | flops 3541565440 | bytes 22642688 | tf_op jit(solution)/shard_map/dot_general | solution.py:33
  304.9 8.0 %fusion.91 = f32[1024,1536]{1,0:T(8,128)S(1)} fusion(bf16[1024,1120]{0,1:T(8,128)(2,1)S(1)} %get-tuple-element.35, bf16[1536,1120]{0,1:T(8,128)(2,1)} %dynamic_update_slice.126), kind=kOutput, calls=%fused_computation.210 | convolution fusion | flops 3523215360 | bytes 12025856 | tf_op jit(solution)/shard_map/dot_general | solution.py:33
  312.9 7.9 %add_convert_fusion = bf16[1024,1536]{1,0:T(8,128)(2,1)} fusion(f32[1024,1536]{1,0:T(8,128)S(1)} %fusion.91, bf16[1024,1120]{0,1:T(8,128)(2,1)S(1)} %get-tuple-element.34, bf16[1536,1120]{0,1:T(8,128)(2,1)} %dynamic_update_slice.121), kind=kOutput, calls=%fused_computation.6 | convolution fusion | flops 3526361088 | bytes 15171584 | tf_op jit(solution)/shard_map/dot_general | solution.py:33
  320.8 6.5 %fusion.10 = f32[1120,1536]{1,0:T(8,128)S(1)} fusion(bf16[1024,1120]{0,1:T(8,128)(2,1)} %get-tuple-element.36, bf16[1,1024,1536]{2,1,0:T(8,128)(2,1)} %all-gather.12.cloned.1.call-done), kind=kOutput, calls=%fused_computation.22 | convolution fusion | flops 3523215360 | bytes 12320768 | tf_op jit(solution)/shard_map/dot_general | solution.py:33
  346.5 17.0 %reduce-scatter.6.cloned.1.call-done = bf16[128,1536]{1,0:T(8,128)(2,1)} async-done(((bf16[1024,1536]{1,0:T(8,128)(2,1)}), bf16[128,1536]{1,0:T(8,128)(2,1)}) %reduce-scatter.6.cloned.1.call-update) | async-done | bytes 393232 | tf_op jit(solution)/shard_map/reduce_scatter | solution.py:308
  368.5 4.7 convolution_convert_fusion.3.do_ref
  373.2 10.7 %attend_back.1 = (bf16[128,1536]{1,0:T(8,128)(2,1)}, f32[1024,256]{1,0:T(8,128)}, f32[1024,256]{1,0:T(8,128)}) custom-call(bf16[128,1536]{1,0:T(8,128)(2,1)} %get-tuple-element.19.q_ref, bf16[1024,256]{1,0:T(8,128)(2,1)} %get-tuple-element.20.k_ref, bf16[1024,256]{1,0:T(8,128)(2,1)} %get-tuple-element.21.v_ref, ...), custom_call_target="tpu_custom_call" | custom-call | flops 2013265920 | bytes 4194304 | tf_op jit(solution)/shard_map/attend_back/pallas_call | solution.py:204
  399.7 4.4 fusion.50
  405.3 7.7 %convolution_convert_fusion = bf16[1024,1536]{1,0:T(8,128)(2,1)} fusion(bf16[1024,1120]{0,1:T(8,128)(2,1)S(1)} %copy-done.50, bf16[1120,1536]{1,0:T(8,128)(2,1)} %dynamic_update_slice.131), kind=kOutput, calls=%fused_computation.20 | convolution fusion | flops 3524788224 | bytes 8880128 | tf_op jit(solution)/shard_map/dot_general | solution.py:33
  427.6 4.4 fusion.60
  463.9 4.2 collective-permute-done.31
  491.5 4.3 all-to-all-start.1
  504.2 7.0 %all-to-all-done.1 = bf16[8,128,256]{2,1,0:T(8,128)(2,1)} async-done(((bf16[8,128,256]{2,1,0:T(8,128)(2,1)}), bf16[8,128,256]{2,1,0:T(8,128)(2,1)}, u32[]{:S(2)}, u32[]{:S(2)}) %all-to-all-start.1) | async-done | bytes 524320 | tf_op jit(solution)/shard_map/all_to_all | solution.py:362
  511.2 4.3 all-to-all-start.4
  518.6 4.8 copy.117
  538.2 5.6 fusion.46
  548.6 9.0 %all-to-all-done.4 = bf16[8,2,48,1120]{3,2,1,0:T(8,128)(2,1)} async-done(((bf16[8,2,48,1120]{3,2,1,0:T(8,128)(2,1)}), bf16[8,2,48,1120]{3,2,1,0:T(8,128)(2,1)}, u32[]{:S(2)}, u32[]{:S(2)}) %all-to-all-start.4) | async-done | bytes 1720352 | tf_op jit(solution)/shard_map/all_to_all | solution.py:338
  562.7 4.7 all-to-all-done
  599.8 9.9 %all-to-all-done.3 = bf16[32,48,448]{2,1,0:T(8,128)(2,1)} async-done(((bf16[32,48,448]{2,1,0:T(8,128)(2,1)}), bf16[32,48,448]{2,1,0:T(8,128)(2,1)}, u32[]{:S(2)}, u32[]{:S(2)}) %all-to-all-start.3) | async-done | bytes 1376288 | tf_op jit(solution)/shard_map/all_to_all | solution.py:369
  (386 shorter events, 342.3 us)
Async XLA Ops:
  7.2 83.7 %all-gather.10.cloned.1.call-start = ((), (), s32[]{:S(2)}) async-start(), calls=%async_computation.12 | async-start | bytes 3538944 | tf_op jit(solution)/shard_map/all_gather | solution.py:282
  8.0 248.5 %all-gather.12.cloned.1.call-start = ((), (), s32[]{:S(2)}) async-start(), calls=%async_computation.13 | async-start | bytes 3538944 | tf_op jit(solution)/shard_map/all_gather | solution.py:283
  10.1 46.5 %collective-permute-start = (bf16[192,2048]{1,0:T(8,128)(2,1)}, bf16[192,2048]{1,0:T(8,128)(2,1)S(1)}, u32[]{:S(2)}, u32[]{:S(2)}) collective-permute-start(bf16[192,2048]{1,0:T(8,128)(2,1)} %constant_dynamic-slice_fusion.10), channel_id=1, source_target_pairs={{0,8},{8,0},{16,24},{24,16},{1,9},{9,1},{17,25},{25,17},{2,10},{10... | collective-permute-start | bytes 2359304 | tf_op jit(solution)/shard_map/ppermute | solution.py:29
  13.1 51.4 %collective-permute-start.2 = (bf16[192,2048]{1,0:T(8,128)(2,1)}, bf16[192,2048]{1,0:T(8,128)(2,1)S(1)}, u32[]{:S(2)}, u32[]{:S(2)}) collective-permute-start(bf16[192,2048]{1,0:T(8,128)(2,1)} %constant_dynamic-slice_fusion.10), channel_id=1, source_target_pairs={{0,16},{8,24},{16,0},{24,8},{1,17},{9,25},{17,1},{25,9},{2,18},{10... | collective-permute-start | bytes 2359304 | tf_op jit(solution)/shard_map/ppermute | solution.py:29
  16.5 116.5 %collective-permute-start.8 = (bf16[192,1536]{1,0:T(8,128)(2,1)}, bf16[192,1536]{1,0:T(8,128)(2,1)}, u32[]{:S(2)}, u32[]{:S(2)}) collective-permute-start(bf16[192,1536]{1,0:T(8,128)(2,1)} %constant_dynamic-slice_fusion.9), channel_id=1, source_target_pairs={{0,8},{8,0},{16,24},{24,16},{1,9},{9,1},{17,25},{25,17},{2,10},{10... | collective-permute-start | bytes 1769480 | tf_op jit(solution)/shard_map/ppermute | solution.py:29
  17.1 248.2 %all-gather.8.cloned.1.call-start = ((), (), s32[]{:S(2)}) async-start(), calls=%async_computation.8 | async-start | bytes 3538944 | tf_op jit(solution)/shard_map/all_gather | solution.py:293
  75.7 62.5 %collective-permute-start.10 = (bf16[192,1536]{1,0:T(8,128)(2,1)}, bf16[192,1536]{1,0:T(8,128)(2,1)}, u32[]{:S(2)}, u32[]{:S(2)}) collective-permute-start(bf16[192,1536]{1,0:T(8,128)(2,1)} %constant_dynamic-slice_fusion.9), channel_id=1, source_target_pairs={{0,16},{8,24},{16,0},{24,8},{1,17},{9,25},{17,1},{25,9},{2,18},{10... | collective-permute-start | bytes 1769480 | tf_op jit(solution)/shard_map/ppermute | solution.py:29
  107.1 256.3 %reduce-scatter.6.cloned.1.call-start = ((), (), s32[]{:S(2)}) async-start(), calls=%async_computation.10 | async-start | bytes 3538944 | tf_op jit(solution)/shard_map/reduce_scatter | solution.py:308
  110.9 29.6 %collective-permute-start.16 = (bf16[384,1120]{0,1:T(8,128)(2,1)}, bf16[384,1120]{0,1:T(8,128)(2,1)}, u32[]{:S(2)}, u32[]{:S(2)}) collective-permute-start(bf16[384,1120]{0,1:T(8,128)(2,1)} %get-tuple-element.59), channel_id=1, source_target_pairs={{0,8},{8,0},{16,24},{24,16},{1,9},{9,1},{17,25},{25,17},{2,10},{10... | collective-permute-start | bytes 2580488 | tf_op jit(solution)/shard_map/ppermute | solution.py:29
  111.5 42.9 %collective-permute-start.17 = (bf16[384,1120]{0,1:T(8,128)(2,1)}, bf16[384,1120]{0,1:T(8,128)(2,1)}, u32[]{:S(2)}, u32[]{:S(2)}) collective-permute-start(bf16[384,1120]{0,1:T(8,128)(2,1)} %get-tuple-element.59), channel_id=1, source_target_pairs={{0,16},{8,24},{16,0},{24,8},{1,17},{9,25},{17,1},{25,9},{2,18},{10... | collective-permute-start | bytes 2580488 | tf_op jit(solution)/shard_map/ppermute | solution.py:29
  133.1 36.9 %collective-permute-start.24 = (bf16[280,1536]{1,0:T(8,128)(2,1)}, bf16[280,1536]{1,0:T(8,128)(2,1)S(1)}, u32[]{:S(2)}, u32[]{:S(2)}) collective-permute-start(bf16[280,1536]{1,0:T(8,128)(2,1)} %get-tuple-element.33), channel_id=1, source_target_pairs={{0,8},{8,0},{16,24},{24,16},{1,9},{9,1},{17,25},{25,17},{2,10},{10... | collective-permute-start | bytes 2580488 | tf_op jit(solution)/shard_map/ppermute | solution.py:29
  138.2 37.6 %collective-permute-start.21 = (bf16[384,1120]{0,1:T(8,128)(2,1)}, bf16[384,1120]{0,1:T(8,128)(2,1)}, u32[]{:S(2)}, u32[]{:S(2)}) collective-permute-start(bf16[384,1120]{0,1:T(8,128)(2,1)} %get-tuple-element.61), channel_id=1, source_target_pairs={{0,16},{8,24},{16,0},{24,8},{1,17},{9,25},{17,1},{25,9},{2,18},{10... | collective-permute-start | bytes 2580488 | tf_op jit(solution)/shard_map/ppermute | solution.py:29
  140.5 38.5 %collective-permute-start.25 = (bf16[280,1536]{1,0:T(8,128)(2,1)}, bf16[280,1536]{1,0:T(8,128)(2,1)}, u32[]{:S(2)}, u32[]{:S(2)}) collective-permute-start(bf16[280,1536]{1,0:T(8,128)(2,1)} %get-tuple-element.33), channel_id=1, source_target_pairs={{0,16},{8,24},{16,0},{24,8},{1,17},{9,25},{17,1},{25,9},{2,18},{10... | collective-permute-start | bytes 2580488 | tf_op jit(solution)/shard_map/ppermute | solution.py:29
  151.6 51.3 %collective-permute-start.12 = (bf16[96,1536]{1,0:T(8,128)(2,1)}, bf16[96,1536]{1,0:T(8,128)(2,1)}, u32[]{:S(2)}, u32[]{:S(2)}) collective-permute-start(bf16[96,1536]{1,0:T(8,128)(2,1)} %slice.213), channel_id=1, source_target_pairs={{0,16},{8,24},{16,0},{24,8},{1,17},{9,25},{17,1},{25,9},{2,18},{10... | collective-permute-start | bytes 884744 | tf_op jit(solution)/shard_map/ppermute | solution.py:29
  154.5 49.1 %collective-permute-start.14 = (bf16[96,1536]{1,0:T(8,128)(2,1)}, bf16[96,1536]{1,0:T(8,128)(2,1)}, u32[]{:S(2)}, u32[]{:S(2)}) collective-permute-start(bf16[96,1536]{1,0:T(8,128)(2,1)} %slice.214), channel_id=1, source_target_pairs={{0,8},{8,0},{16,24},{24,16},{1,9},{9,1},{17,25},{25,17},{2,10},{10... | collective-permute-start | bytes 884744 | tf_op jit(solution)/shard_map/ppermute | solution.py:29
  179.0 31.5 %collective-permute-start.18 = (bf16[192,1120]{1,0:T(8,128)(2,1)}, bf16[192,1120]{1,0:T(8,128)(2,1)}, u32[]{:S(2)}, u32[]{:S(2)}) collective-permute-start(bf16[192,1120]{1,0:T(8,128)(2,1)} %copy.104), channel_id=1, source_target_pairs={{0,16},{8,24},{16,0},{24,8},{1,17},{9,25},{17,1},{25,9},{2,18},{10... | collective-permute-start | bytes 1290248 | tf_op jit(solution)/shard_map/ppermute | solution.py:29
  197.6 34.2 %collective-permute-start.19 = (bf16[192,1120]{1,0:T(8,128)(2,1)}, bf16[192,1120]{1,0:T(8,128)(2,1)}, u32[]{:S(2)}, u32[]{:S(2)}) collective-permute-start(bf16[192,1120]{1,0:T(8,128)(2,1)} %copy.106), channel_id=1, source_target_pairs={{0,8},{8,0},{16,24},{24,16},{1,9},{9,1},{17,25},{25,17},{2,10},{10... | collective-permute-start | bytes 1290248 | tf_op jit(solution)/shard_map/ppermute | solution.py:29
  207.7 33.3 %collective-permute-start.23 = (bf16[192,1120]{1,0:T(8,128)(2,1)}, bf16[192,1120]{1,0:T(8,128)(2,1)}, u32[]{:S(2)}, u32[]{:S(2)}) collective-permute-start(bf16[192,1120]{1,0:T(8,128)(2,1)} %copy.114), channel_id=1, source_target_pairs={{0,8},{8,0},{16,24},{24,16},{1,9},{9,1},{17,25},{25,17},{2,10},{10... | collective-permute-start | bytes 1290248 | tf_op jit(solution)/shard_map/ppermute | solution.py:29
  209.9 40.1 %collective-permute-start.26 = (bf16[140,1536]{1,0:T(8,128)(2,1)}, bf16[140,1536]{1,0:T(8,128)(2,1)}, u32[]{:S(2)}, u32[]{:S(2)}) collective-permute-start(bf16[140,1536]{1,0:T(8,128)(2,1)} %slice.220), channel_id=1, source_target_pairs={{0,16},{8,24},{16,0},{24,8},{1,17},{9,25},{17,1},{25,9},{2,18},{10... | collective-permute-start | bytes 1290248 | tf_op jit(solution)/shard_map/ppermute | solution.py:29
  210.5 43.0 %collective-permute-start.27 = (bf16[140,1536]{1,0:T(8,128)(2,1)}, bf16[140,1536]{1,0:T(8,128)(2,1)}, u32[]{:S(2)}, u32[]{:S(2)}) collective-permute-start(bf16[140,1536]{1,0:T(8,128)(2,1)} %slice.221), channel_id=1, source_target_pairs={{0,8},{8,0},{16,24},{24,16},{1,9},{9,1},{17,25},{25,17},{2,10},{10... | collective-permute-start | bytes 1290248 | tf_op jit(solution)/shard_map/ppermute | solution.py:29
  320.8 158.3 %reduce-scatter.8.cloned.1.call-start = ((), (), s32[]{:S(2)}) async-start(), calls=%async_computation.11 | async-start | bytes 1179648 | tf_op jit(solution)/shard_map/reduce_scatter | solution.py:352
  328.4 199.7 %collective-permute-start.36 = (bf16[140,1536]{1,0:T(8,128)(2,1)}, bf16[140,1536]{1,0:T(8,128)(2,1)}, u32[]{:S(2)}, u32[]{:S(2)}) collective-permute-start(bf16[140,1536]{1,0:T(8,128)(2,1)} %get-tuple-element.53), channel_id=1, source_target_pairs={{0,16},{8,24},{16,0},{24,8},{1,17},{9,25},{17,1},{25,9},{2,18},{10... | collective-permute-start | bytes 1290248 | tf_op jit(solution)/shard_map/ppermute | solution.py:29
  330.9 197.2 %collective-permute-start.38 = (bf16[140,1536]{1,0:T(8,128)(2,1)}, bf16[140,1536]{1,0:T(8,128)(2,1)}, u32[]{:S(2)}, u32[]{:S(2)}) collective-permute-start(bf16[140,1536]{1,0:T(8,128)(2,1)} %get-tuple-element.54), channel_id=1, source_target_pairs={{0,8},{8,0},{16,24},{24,16},{1,9},{9,1},{17,25},{25,17},{2,10},{10... | collective-permute-start | bytes 1290248 | tf_op jit(solution)/shard_map/ppermute | solution.py:29
  387.6 208.3 %reduce-scatter.4.cloned.1.call-start = ((), (), s32[]{:S(2)}) async-start(), calls=%async_computation.9 | async-start | bytes 3538944 | tf_op jit(solution)/shard_map/reduce_scatter | solution.py:310
  392.6 39.4 %collective-permute-start.28 = (bf16[192,1120]{1,0:T(8,128)(2,1)}, bf16[192,1120]{1,0:T(8,128)(2,1)}, u32[]{:S(2)}, u32[]{:S(2)}) collective-permute-start(bf16[192,1120]{1,0:T(8,128)(2,1)} %copy.124), channel_id=1, source_target_pairs={{0,16},{8,24},{16,0},{24,8},{1,17},{9,25},{17,1},{25,9},{2,18},{10... | collective-permute-start | bytes 1290248 | tf_op jit(solution)/shard_map/ppermute | solution.py:29
  398.2 40.8 %collective-permute-start.30 = (bf16[192,1120]{1,0:T(8,128)(2,1)}, bf16[192,1120]{1,0:T(8,128)(2,1)}, u32[]{:S(2)}, u32[]{:S(2)}) collective-permute-start(bf16[192,1120]{1,0:T(8,128)(2,1)} %copy.126), channel_id=1, source_target_pairs={{0,8},{8,0},{16,24},{24,16},{1,9},{9,1},{17,25},{25,17},{2,10},{10... | collective-permute-start | bytes 1290248 | tf_op jit(solution)/shard_map/ppermute | solution.py:29
  454.0 41.9 %collective-permute-start.33 = (bf16[384,1120]{0,1:T(8,128)(2,1)}, bf16[384,1120]{0,1:T(8,128)(2,1)}, u32[]{:S(2)}, u32[]{:S(2)}) collective-permute-start(bf16[384,1120]{0,1:T(8,128)(2,1)} %pad_maximum_fusion.6), channel_id=1, source_target_pairs={{0,8},{8,0},{16,24},{24,16},{1,9},{9,1},{17,25},{25,17},{2,10},{10... | collective-permute-start | bytes 2580488 | tf_op jit(solution)/shard_map/ppermute | solution.py:29
  462.5 33.4 %collective-permute-start.35 = (bf16[384,1120]{0,1:T(8,128)(2,1)}, bf16[384,1120]{0,1:T(8,128)(2,1)}, u32[]{:S(2)}, u32[]{:S(2)}) collective-permute-start(bf16[384,1120]{0,1:T(8,128)(2,1)} %pad_maximum_fusion.7), channel_id=1, source_target_pairs={{0,16},{8,24},{16,0},{24,8},{1,17},{9,25},{17,1},{25,9},{2,18},{10... | collective-permute-start | bytes 2580488 | tf_op jit(solution)/shard_map/ppermute | solution.py:29
  511.2 46.3 %all-to-all-start.4 = ((bf16[8,2,48,1120]{3,2,1,0:T(8,128)(2,1)}), bf16[8,2,48,1120]{3,2,1,0:T(8,128)(2,1)}, u32[]{:S(2)}, u32[]{:S(2)}) async-start(bf16[8,2,48,1120]{3,2,1,0:T(8,128)(2,1)} %copy.134), calls=%async_computation.7 | async-start | bytes 3538944 | tf_op jit(solution)/shard_map/all_to_all | solution.py:338
  531.2 39.8 %collective-permute-start.37 = (bf16[280,1536]{1,0:T(8,128)(2,1)}, bf16[280,1536]{1,0:T(8,128)(2,1)S(1)}, u32[]{:S(2)}, u32[]{:S(2)}) collective-permute-start(bf16[280,1536]{1,0:T(8,128)(2,1)} %pad_maximum_fusion.8), channel_id=1, source_target_pairs={{0,8},{8,0},{16,24},{24,16},{1,9},{9,1},{17,25},{25,17},{2,10},{10... | collective-permute-start | bytes 2580488 | tf_op jit(solution)/shard_map/ppermute | solution.py:29
  532.2 38.8 %collective-permute-start.39 = (bf16[280,1536]{1,0:T(8,128)(2,1)}, bf16[280,1536]{1,0:T(8,128)(2,1)}, u32[]{:S(2)}, u32[]{:S(2)}) collective-permute-start(bf16[280,1536]{1,0:T(8,128)(2,1)} %pad_maximum_fusion.9), channel_id=1, source_target_pairs={{0,16},{8,24},{16,0},{24,8},{1,17},{9,25},{17,1},{25,9},{2,18},{10... | collective-permute-start | bytes 2580488 | tf_op jit(solution)/shard_map/ppermute | solution.py:29
  567.4 42.4 %all-to-all-start.3 = ((bf16[32,48,448]{2,1,0:T(8,128)(2,1)}), bf16[32,48,448]{2,1,0:T(8,128)(2,1)}, u32[]{:S(2)}, u32[]{:S(2)}) async-start(bf16[32,48,448]{2,1,0:T(8,128)(2,1)} %pad_maximum_fusion), calls=%async_computation.6 | async-start | bytes 3145728 | tf_op jit(solution)/shard_map/all_to_all | solution.py:369
  (72 other events, 604.9 us)
Sparse Core Ops, SparseCore 0:
  9.7 40.9 all-gather.9
  52.3 37.0 all-gather.11
  107.2 38.5 all-gather.7
  320.9 42.5 reduce-scatter.5
  387.7 31.8 reduce-scatter.7
  427.7 37.9 reduce-scatter.3
